TPU v7x, 256 devices: a whole 4x4x8 slice. The times are simulated.
256 devices in a mesh: lat: 4 (over z_lo, core), lon: 16 (over z_hi, y), tm: 4 (over x).
Axes of the slice: x: 4, y: 4, z: 8 (z_hi: 4, z_lo: 2; z = z_hi * 2 + z_lo), core: 2. Of those that a mesh axis runs over, the one named last changes fastest.
Arguments:
- signal: bfloat16 [4, 78, 32, 2048], P('tm', None, 'lat', 'lon'), may hold values from -6 to 6
- dictionary: bfloat16 [64, 9984], P('lon'), may hold values from -0.0625 to 0.0625
- codes_init: float32 [4, 64, 8, 512], P('tm', None, 'lat', 'lon'), may hold values from -3 to 3
- thresholds: float32 [64], replicated, may hold values from 0.2 to 2
Outputs:
- codes: float32 [4, 64, 8, 512], P('tm', None, 'lat', 'lon')
- dict_grad: float32 [64, 9984], P('lon')
All inputs are finite; a program needn't handle non-finite values.
Results may differ from a plain program's by a relative error of at most 0.0044.
Values may be sent and summed in bfloat16 or wider, within the bound.
No kernel may reach another device: no remote copies, remote signals or barrier semaphores. Data moves between devices by JAX's collectives and lax.ppermute only.
A program may use at most 128 MiB of HBM per device.

v0:
```python
import math
import jax
import jax.numpy as jnp
from jax import lax
from jax.sharding import PartitionSpec as P

ITERS = 2
STEP_SIZE = 0.5


def passed_along(shard, axis, by):
    peers = lax.axis_size(axis)
    pairs = [(i, i + by) for i in range(peers) if 0 <= i + by < peers]
    return lax.ppermute(shard, axis, pairs)


def shifted(block, axis, distance):
    devices = range(lax.axis_size(axis))
    route = [((i - distance) % len(devices), i) for i in devices]
    return lax.ppermute(block, axis, route)


def combos():
    return [(delay, down, right) for delay in (0, 1) for down in (0, 1) for right in (0, 1)]


def to_atoms(local, channels, count):
    shaped = local.reshape(channels, 4, 4, 2, 2, 2, count)
    return shaped.transpose(6, 3, 0, 4, 1, 5, 2).reshape(count, 2 * channels * 64)


def extend_codes(coded):
    atoms, rows, columns = coded.shape
    earlier = passed_along(coded, "tm", 1)
    both = jnp.stack([coded, earlier])
    above = passed_along(both[:, :, -1:, :], "lat", 1)
    both = jnp.concatenate([above, both], axis=2)
    beside = shifted(both[:, :, :, -1:], "lon", 1)
    both = jnp.concatenate([beside, both], axis=3)
    pieces = [
        both[delay, :, 1 - down : 1 - down + rows, 1 - right : 1 - right + columns]
        for delay, down, right in combos()
    ]
    return jnp.stack(pieces).reshape(8 * atoms, rows * columns)


def body(signal, dictionary, codes_init, thresholds):
    channels = signal.shape[1]
    rows = signal.shape[2] // 4
    columns = signal.shape[3] // 4
    patch = channels * 16
    gathered = lax.all_gather(dictionary, "lon", axis=0, tiled=True)
    atoms = gathered.shape[0]
    blocks = (
        gathered.reshape(atoms, 2, channels, 2, 4, 2, 4)
        .transpose(1, 3, 5, 2, 4, 6, 0)
        .reshape(8, patch, atoms)
    )
    synth_matrix = blocks.transpose(1, 0, 2).reshape(patch, 8 * atoms)
    target = (
        signal[0]
        .reshape(channels, rows, 4, columns, 4)
        .transpose(0, 2, 4, 1, 3)
        .reshape(patch, rows * columns)
    )

    def residual_of(current):
        stacked = extend_codes(current.astype(jnp.bfloat16).reshape(atoms, rows, columns))
        synth = jnp.dot(synth_matrix, stacked, preferred_element_type=jnp.float32)
        return ((synth - target).astype(jnp.bfloat16), stacked)

    adjoint_matrix = blocks.transpose(2, 0, 1).reshape(atoms, 8 * patch)
    current = codes_init[0].reshape(atoms, rows * columns)
    moving = current
    momentum_now = 1.0
    shrink = STEP_SIZE * thresholds[:, None]
    for turn in range(ITERS):
        residual, stacked = residual_of(moving)
        frame = residual.reshape(patch, rows, columns)
        later = passed_along(frame, "tm", -1)
        both = jnp.stack([frame, later])
        below = passed_along(both[:, :, :1, :], "lat", -1)
        both = jnp.concatenate([both, below], axis=2)
        beside = shifted(both[:, :, :, :1], "lon", -1)
        both = jnp.concatenate([both, beside], axis=3)
        pieces = [
            both[delay, :, down : down + rows, right : right + columns]
            for delay, down, right in combos()
        ]
        adjoint_stacked = jnp.stack(pieces).reshape(8 * patch, rows * columns)
        descent = moving - STEP_SIZE * jnp.dot(
            adjoint_matrix, adjoint_stacked, preferred_element_type=jnp.float32
        )
        updated = jnp.sign(descent) * jnp.maximum(jnp.abs(descent) - shrink, 0.0)
        momentum_next = (1.0 + math.sqrt(1.0 + 4.0 * momentum_now * momentum_now)) / 2.0
        moving = updated + (momentum_now - 1.0) / momentum_next * (updated - current)
        current = updated
        momentum_now = momentum_next
    residual, stacked = residual_of(current)
    positions = lax.axis_size("tm") * lax.axis_size("lat") * lax.axis_size("lon") * rows * columns
    scale = 1.0 / math.sqrt(positions)
    owned_rows = atoms // lax.axis_size("lon")
    local = lax.dot_general(
        residual, stacked, (((1,), (1,)), ((), ())), preferred_element_type=jnp.float32
    )
    total = lax.psum(to_atoms(local, channels, atoms) * scale, ("lat", "lon", "tm"))
    mine = lax.dynamic_slice_in_dim(total, lax.axis_index("lon") * owned_rows, owned_rows, 0)
    return (current.reshape(1, atoms, rows, columns), mine)


def solution(mesh):
    placed = (P("tm", None, "lat", "lon"), P("lon", None), P("tm", None, "lat", "lon"), P())
    return jax.shard_map(
        body,
        mesh=mesh,
        in_specs=placed,
        out_specs=(P("tm", None, "lat", "lon"), P("lon", None)),
        check_vma=False,
    )
```

profile of v0, /device:TPU:2, one launch (start us, length us, event | category | flops | bytes accessed | tf_op | source)
XLA Modules:
  0.0 632.7 jit_solution(5299699721707933311)
XLA Ops:
  8.7 3.4 collective-permute-start
  12.1 2.2 collective-permute-done
  14.3 1.3 collective-permute-start.1
  15.6 0.8 collective-permute-done.1
  16.5 1.6 collective-permute-start.2
  18.1 1.1 copy.73
  19.2 1.4 copy.53
  21.6 5.3 collective-permute-done.2
  27.2 40.2 %all-gather.3.cloned.1.call-done = bf16[16,4,9984]{2,1,0:T(4,128)(2,1)} async-done(((bf16[1,4,9984]{2,1,0:T(4,128)(2,1)}), bf16[16,4,9984]{2,1,0:T(4,128)(2,1)}) %all-gather.3.cloned.1.call-update) | async-done | bytes 1277968 | tf_op jit(solution)/shard_map/all_gather | solution.py:52
  67.5 89.3 %reshape.84 = bf16[64,2,78,2,4,2,4]{6,5,4,3,2,1,0:T(2,128)(2,1)} reshape(bf16[16,4,9984]{2,1,0:T(4,128)(2,1)} %all-gather.3.cloned.1.call-done) | data formatting | bytes 2555904 | tf_op jit(solution)/shard_map/reshape | solution.py:55
  156.8 86.1 %copy.69 = bf16[64,2,78,2,4,2,4]{0,6,4,2,5,3,1:T(4,128)(2,1)S(1)} copy(bf16[64,2,78,2,4,2,4]{6,5,4,3,2,1,0:T(2,128)(2,1)} %reshape.84) | data formatting | bytes 2555904 | tf_op jit(solution)/shard_map/transpose | solution.py:56
  242.8 2.8 copy.51
  245.6 1.7 fusion.3
  247.3 2.5 collective-permute-start.3
  249.8 4.7 collective-permute-done.3
  254.6 1.3 collective-permute-start.4
  255.9 2.0 collective-permute-done.4
  257.9 3.9 collective-permute-start.5
  261.8 1.6 collective-permute-done.5
  263.7 1.8 copy.55
  265.5 3.5 reshape.68
  269.0 1.9 fusion.15
  270.9 3.4 collective-permute-start.6
  274.3 2.2 collective-permute-done.6
  276.5 2.2 collective-permute-start.7
  278.7 0.8 collective-permute-done.7
  279.6 8.1 %collective-permute-done.8 = bf16[2,64,3,1]{1,3,2,0:T(2,128)(2,1)S(1)} collective-permute-done((bf16[2,64,3,1]{1,3,2,0:T(2,128)(2,1)S(1)}, bf16[2,64,3,1]{1,3,2,0:T(2,128)(2,1)S(1)}, u32[]{:S(2)}, u32[]{:S(2)}) %collective-permute-start.8) | collective-permute-done | bytes 800 | tf_op jit(solution)/shard_map/ppermute | solution.py:20
  288.1 1.7 fusion.4
  289.8 1.9 collective-permute-start.9
  291.7 6.9 %collective-permute-done.9 = bf16[1248,2,32]{0,2,1:T(8,128)(2,1)S(1)} collective-permute-done((bf16[1248,2,32]{0,2,1:T(8,128)(2,1)S(1)}, bf16[1248,2,32]{0,2,1:T(8,128)(2,1)S(1)}, u32[]{:S(2)}, u32[]{:S(2)}) %collective-permute-start.9) | collective-permute-done | bytes 159776 | tf_op jit(solution)/shard_map/ppermute | solution.py:14
  298.7 1.3 collective-permute-start.10
  300.0 2.0 collective-permute-done.10
  302.0 2.2 collective-permute-start.11
  304.2 1.9 collective-permute-done.11
  306.5 1.8 copy.58
  308.3 3.5 reshape.73
  311.7 2.5 fusion.16
  314.3 3.4 collective-permute-start.12
  317.7 2.2 collective-permute-done.12
  319.9 4.1 collective-permute-start.13
  324.1 0.8 collective-permute-done.13
  325.0 7.8 %collective-permute-done.14 = bf16[2,64,3,1]{1,3,2,0:T(2,128)(2,1)S(1)} collective-permute-done((bf16[2,64,3,1]{1,3,2,0:T(2,128)(2,1)S(1)}, bf16[2,64,3,1]{1,3,2,0:T(2,128)(2,1)S(1)}, u32[]{:S(2)}, u32[]{:S(2)}) %collective-permute-start.14) | collective-permute-done | bytes 800 | tf_op jit(solution)/shard_map/ppermute | solution.py:20
  333.2 1.7 fusion.5
  335.1 2.7 multiply_bitcast_fusion
  337.8 7.9 %copy.64 = f32[64,2,78,2,4,2,4]{0,6,5,4,3,2,1:T(4,128)} copy(f32[64,2,78,2,4,2,4]{2,0,5,3,1,6,4:T(8,128)} %multiply_bitcast_fusion) | data formatting | bytes 5111808 | tf_op jit(solution)/shard_map/mul | solution.py:106
  345.7 271.5 %all-reduce.2.cloned.1.call-done = f32[64,9984]{0,1:T(8,128)} async-done(((f32[64,9984]{0,1:T(8,128)}), f32[64,9984]{0,1:T(8,128)}) %all-reduce.2.cloned.1.call-update) | async-done | bytes 2555920 | tf_op jit(solution)/shard_map/psum | solution.py:106
  617.2 4.7 constant_dynamic-slice_fusion
  621.9 3.9 copy.65
  (75 shorter events, 4.6 us)
Async XLA Ops:
  7.2 60.3 %all-gather.3.cloned.1.call-start = ((), (), s32[]{:S(2)}) async-start(), calls=%async_computation.1 | async-start | bytes 1357824 | tf_op jit(solution)/shard_map/all_gather | solution.py:52
  7.9 609.3 %all-reduce.2.cloned.1.call-start = ((), (), s32[]{:S(2)}) async-start(), calls=%async_computation | async-start | bytes 10223616 | tf_op jit(solution)/shard_map/psum | solution.py:106
  8.7 5.6 collective-permute-start
  14.3 2.1 collective-permute-start.1
  16.5 10.4 %collective-permute-start.2 = (bf16[2,64,3,1]{1,3,2,0:T(2,128)(2,1)S(1)}, bf16[2,64,3,1]{1,3,2,0:T(2,128)(2,1)S(1)}, u32[]{:S(2)}, u32[]{:S(2)}) collective-permute-start(bf16[2,64,3,1]{1,3,2,0:T(2,128)(2,1)S(1)} %pad_maximum_fusion.21), channel_id=1, source_target_pairs={{60,0},{0,4},{4,8},{8,12},{12,16},{16,20},{20,24},{24,28},{28,32},... | collective-permute-start | bytes 2312 | tf_op jit(solution)/shard_map/ppermute | solution.py:20
  245.6 10.2 %copy-start.1 = (f32[64]{0:T(128)S(1)}, f32[64]{0:T(128)}, u32[]{:S(2)}) copy-start(f32[64]{0:T(128)} %param.7) | copy-start | bytes 772
  247.3 7.2 %collective-permute-start.3 = (bf16[1248,2,32]{0,2,1:T(8,128)(2,1)S(1)}, bf16[1248,2,32]{0,2,1:T(8,128)(2,1)S(1)}, u32[]{:S(2)}, u32[]{:S(2)}) collective-permute-start(bf16[1248,2,32]{0,2,1:T(8,128)(2,1)S(1)} %bitcast.120), channel_id=1, source_target_pairs={{1,0},{2,1},{3,2},{5,4},{6,5},{7,6},{9,8},{10,9},{11,10},{13,12},{... | collective-permute-start | bytes 479240 | tf_op jit(solution)/shard_map/ppermute | solution.py:14
  254.6 3.3 collective-permute-start.4
  257.9 5.5 collective-permute-start.5
  265.5 3.5 copy-start
  270.9 5.6 collective-permute-start.6
  276.5 3.0 collective-permute-start.7
  279.5 8.2 %collective-permute-start.8 = (bf16[2,64,3,1]{1,3,2,0:T(2,128)(2,1)S(1)}, bf16[2,64,3,1]{1,3,2,0:T(2,128)(2,1)S(1)}, u32[]{:S(2)}, u32[]{:S(2)}) collective-permute-start(bf16[2,64,3,1]{1,3,2,0:T(2,128)(2,1)S(1)} %pad_maximum_fusion.20), channel_id=1, source_target_pairs={{60,0},{0,4},{4,8},{8,12},{12,16},{16,20},{20,24},{24,28},{28,32},... | collective-permute-start | bytes 2312 | tf_op jit(solution)/shard_map/ppermute | solution.py:20
  289.8 8.9 %collective-permute-start.9 = (bf16[1248,2,32]{0,2,1:T(8,128)(2,1)S(1)}, bf16[1248,2,32]{0,2,1:T(8,128)(2,1)S(1)}, u32[]{:S(2)}, u32[]{:S(2)}) collective-permute-start(bf16[1248,2,32]{0,2,1:T(8,128)(2,1)S(1)} %bitcast.127), channel_id=1, source_target_pairs={{1,0},{2,1},{3,2},{5,4},{6,5},{7,6},{9,8},{10,9},{11,10},{13,12},{... | collective-permute-start | bytes 479240 | tf_op jit(solution)/shard_map/ppermute | solution.py:14
  298.7 3.3 collective-permute-start.10
  302.0 4.2 collective-permute-start.11
  314.3 5.6 collective-permute-start.12
  319.9 5.0 collective-permute-start.13
  324.9 7.9 %collective-permute-start.14 = (bf16[2,64,3,1]{1,3,2,0:T(2,128)(2,1)S(1)}, bf16[2,64,3,1]{1,3,2,0:T(2,128)(2,1)S(1)}, u32[]{:S(2)}, u32[]{:S(2)}) collective-permute-start(bf16[2,64,3,1]{1,3,2,0:T(2,128)(2,1)S(1)} %pad_maximum_fusion.19), channel_id=1, source_target_pairs={{60,0},{0,4},{4,8},{8,12},{12,16},{16,20},{20,24},{24,28},{28,32},... | collective-permute-start | bytes 2312 | tf_op jit(solution)/shard_map/ppermute | solution.py:20
Sparse Core Ops, SparseCore 0:
  10.4 57.0 all-gather.2
  345.8 271.3 all-reduce.1
where the time goes:
time: 635 us; the launch traced here: 633 us
  waiting for transfers between devices  362 us (57%)
  local copies, waits for them, and re-layouts  210 us (33%)
  starting transfers between devices  32.7 us (5%)
  between operations  14.5 us (2%)
  matrix products  12.2 us (2%)
    psum x1, waiting for transfers between devices, body(): lax.psum(to_atoms(local, channels, atoms) * scale, ('lat', 'lon', 'tm'))  271 us
    reshape x1, local copies, waits for them, and re-layouts, body(): gathered.reshape(atoms, 2, channels, 2, 4, 2, 4)  89.3 us
    transpose x1, local copies, waits for them, and re-layouts, body(): blocks = gathered.reshape(atoms, 2, channels, 2, 4, 2, 4).transpose(1, 3,...  86.1 us
    all_gather x1, waiting for transfers between devices, body(): gathered = lax.all_gather(dictionary, 'lon', axis=0, tiled=True)  40.2 us
    ppermute x10, starting transfers between devices, passed_along(): return lax.ppermute(shard, axis, pairs)  24.8 us
    ppermute x10, waiting for transfers between devices, passed_along(): return lax.ppermute(shard, axis, pairs)  24.7 us
    ppermute x5, waiting for transfers between devices, shifted(): return lax.ppermute(block, axis, route)  24.7 us
  transfers between devices with their start and end apart: 17, of which 17 were waited for; matrix products, arithmetic and copies ran while one was open for 1% of the time, Pallas kernels for 0%

commit v1 on v0

--- a/solution.py
+++ b/solution.py
@@ -103,7 +103,7 @@
     local = lax.dot_general(
         residual, stacked, (((1,), (1,)), ((), ())), preferred_element_type=jnp.float32
     )
-    total = lax.psum(to_atoms(local, channels, atoms) * scale, ("lat", "lon", "tm"))
+    total = lax.psum(lax.psum(to_atoms(local, channels, atoms) * scale, ("lon", "tm")), "lat")
     mine = lax.dynamic_slice_in_dim(total, lax.axis_index("lon") * owned_rows, owned_rows, 0)
     return (current.reshape(1, atoms, rows, columns), mine)
 

time: 635 us -> 1230 us (1.94)
  waiting for transfers between devices: 362 us -> 955 us
    psum x1 -> x2, waiting for transfers between devices: 271 us -> 864 us  [the longest x1 754 us: body(): lax.psum(to_atoms(local, channels, atoms) * scale, ('lon', 'tm'))]
  transfers between devices with their start and end apart: 17 -> 18, of which waited for: 17 -> 18; matrix products, arithmetic and copies ran while one was open for 1% -> 0% of each run, Pallas kernels for 0% -> 0%
where the time goes in v1:
time: 1230 us
  waiting for transfers between devices  955 us (78%)
  local copies, waits for them, and re-layouts  210 us (17%)
  starting transfers between devices  32.8 us (3%)
  between operations  14.2 us (1%)
    psum x1, waiting for transfers between devices, body(): lax.psum(to_atoms(local, channels, atoms) * scale, ('lon', 'tm'))  754 us
    psum x1, waiting for transfers between devices, body(): lax.psum(lax.psum(to_atoms(local, channels, atoms) * scale, ('lon', 'tm')...  110 us
    reshape x1, local copies, waits for them, and re-layouts, body(): gathered.reshape(atoms, 2, channels, 2, 4, 2, 4)  89.3 us
    transpose x1, local copies, waits for them, and re-layouts, body(): blocks = gathered.reshape(atoms, 2, channels, 2, 4, 2, 4).transpose(1, 3,...  86.1 us
    all_gather x1, waiting for transfers between devices, body(): gathered = lax.all_gather(dictionary, 'lon', axis=0, tiled=True)  40.2 us
    ppermute x10, starting transfers between devices, passed_along(): return lax.ppermute(shard, axis, pairs)  24.8 us
    ppermute x10, waiting for transfers between devices, passed_along(): return lax.ppermute(shard, axis, pairs)  24.7 us
    ppermute x5, waiting for transfers between devices, shifted(): return lax.ppermute(block, axis, route)  24.7 us
  transfers between devices with their start and end apart: 18, of which 18 were waited for; matrix products, arithmetic and copies ran while one was open for 0% of the time, Pallas kernels for 0%

profile of v1, /device:TPU:2, one launch (start us, length us, event | category | flops | bytes accessed | tf_op | source)
XLA Modules:
  0.0 1225.1 jit_solution(17198893567389030809)
XLA Ops:
  8.7 3.4 collective-permute-start
  12.1 2.2 collective-permute-done
  14.3 1.3 collective-permute-start.1
  16.5 1.6 collective-permute-start.2
  18.1 1.1 copy.73
  19.2 1.4 copy.53
  21.6 5.3 collective-permute-done.2
  27.2 40.2 %all-gather.3.cloned.1.call-done = bf16[16,4,9984]{2,1,0:T(4,128)(2,1)} async-done(((bf16[1,4,9984]{2,1,0:T(4,128)(2,1)}), bf16[16,4,9984]{2,1,0:T(4,128)(2,1)}) %all-gather.3.cloned.1.call-update) | async-done | bytes 1277968 | tf_op jit(solution)/shard_map/all_gather | solution.py:52
  67.5 89.3 %reshape.84 = bf16[64,2,78,2,4,2,4]{6,5,4,3,2,1,0:T(2,128)(2,1)} reshape(bf16[16,4,9984]{2,1,0:T(4,128)(2,1)} %all-gather.3.cloned.1.call-done) | data formatting | bytes 2555904 | tf_op jit(solution)/shard_map/reshape | solution.py:55
  156.8 86.1 %copy.69 = bf16[64,2,78,2,4,2,4]{0,6,4,2,5,3,1:T(4,128)(2,1)S(1)} copy(bf16[64,2,78,2,4,2,4]{6,5,4,3,2,1,0:T(2,128)(2,1)} %reshape.84) | data formatting | bytes 2555904 | tf_op jit(solution)/shard_map/transpose | solution.py:56
  242.8 2.8 copy.51
  245.6 1.7 fusion.3
  247.3 2.5 collective-permute-start.3
  249.8 4.7 collective-permute-done.3
  254.6 1.3 collective-permute-start.4
  255.9 2.0 collective-permute-done.4
  257.9 3.9 collective-permute-start.5
  261.8 1.6 collective-permute-done.5
  263.7 1.8 copy.55
  265.5 3.5 reshape.68
  269.0 1.9 fusion.15
  270.9 3.4 collective-permute-start.6
  274.3 2.2 collective-permute-done.6
  276.5 2.2 collective-permute-start.7
  278.7 0.8 collective-permute-done.7
  279.6 8.1 collective-permute-done.8
  288.1 1.7 fusion.4
  289.8 1.9 collective-permute-start.9
  291.7 6.9 collective-permute-done.9
  298.7 1.3 collective-permute-start.10
  300.0 2.0 collective-permute-done.10
  302.0 2.2 collective-permute-start.11
  304.2 1.9 collective-permute-done.11
  306.5 1.8 copy.58
  308.3 3.5 reshape.73
  311.7 2.5 fusion.16
  314.3 3.4 collective-permute-start.12
  317.7 2.2 collective-permute-done.12
  319.9 4.1 collective-permute-start.13
  324.1 0.8 collective-permute-done.13
  325.0 7.8 collective-permute-done.14
  333.2 1.7 fusion.5
  335.1 2.7 multiply_bitcast_fusion
  337.8 7.9 copy.64
  345.8 754.3 %all-reduce.3.cloned.1.call-done = f32[64,9984]{0,1:T(8,128)} async-done(((f32[64,9984]{0,1:T(8,128)}), f32[64,9984]{0,1:T(8,128)}) %all-reduce.3.cloned.1.call-update) | async-done | bytes 2555920 | tf_op jit(solution)/shard_map/psum | solution.py:106
  1100.1 109.9 %all-reduce.5.cloned.1.call-done = f32[64,9984]{0,1:T(8,128)} async-done(((f32[64,9984]{0,1:T(8,128)}), f32[64,9984]{0,1:T(8,128)}) %all-reduce.5.cloned.1.call-update) | async-done | bytes 2555920 | tf_op jit(solution)/shard_map/psum | solution.py:106
  1210.0 4.7 constant_dynamic-slice_fusion
  1214.7 3.9 copy.65
  (78 shorter events, 5.5 us)
Async XLA Ops:
  7.2 60.3 %all-gather.3.cloned.1.call-start = ((), (), s32[]{:S(2)}) async-start(), calls=%async_computation.2 | async-start | bytes 1357824 | tf_op jit(solution)/shard_map/all_gather | solution.py:52
  7.9 1092.2 %all-reduce.3.cloned.1.call-start = ((), (), s32[]{:S(2)}) async-start(), calls=%async_computation | async-start | bytes 10223616 | tf_op jit(solution)/shard_map/psum | solution.py:106
  8.7 5.6 collective-permute-start
  14.3 2.1 collective-permute-start.1
  16.5 10.4 collective-permute-start.2
  245.6 10.2 copy-start.1
  247.3 7.2 collective-permute-start.3
  254.6 3.3 collective-permute-start.4
  257.9 5.5 collective-permute-start.5
  265.5 3.5 copy-start
  270.9 5.6 collective-permute-start.6
  276.5 3.0 collective-permute-start.7
  279.5 8.2 collective-permute-start.8
  289.8 8.9 collective-permute-start.9
  298.7 3.3 collective-permute-start.10
  302.0 4.2 collective-permute-start.11
  314.3 5.6 collective-permute-start.12
  319.9 5.0 collective-permute-start.13
  324.9 7.9 collective-permute-start.14
  345.7 864.3 %all-reduce.5.cloned.1.call-start = ((), (), s32[]{:S(2)}) async-start(), calls=%async_computation.1 | async-start | bytes 10223616 | tf_op jit(solution)/shard_map/psum | solution.py:106
Sparse Core Ops, SparseCore 0:
  10.4 57.0 all-gather.2
  345.8 754.1 all-reduce.2
  1102.8 107.2 all-reduce.4
